TPU v7x, 32 devices: a whole 2x2x4 slice. The times are simulated.
32 devices in a mesh: var: 8 (over y, x, core), head: 4 (over z).
Axes of the slice: x: 2, y: 2, z: 4, core: 2. Of those that a mesh axis runs over, the one named last changes fastest.
Arguments:
- series: float32 [1024, 8192], P('var', 'head'), may hold values from -48 to 48
- emb_weight: float32 [8192, 512], P('head'), as said below
- emb_bias: float32 [512], replicated, may hold values from -3 to 3
- q_weight: float32 [512, 512], P(None, 'head'), may hold values from -0.75 to 0.75
- k_weight: float32 [512, 512], P(None, 'head'), may hold values from -0.25 to 0.25
- v_weight: float32 [512, 512], P(None, 'head'), may hold values from -0.25 to 0.25
- out_weight: float32 [512, 512], P('head'), may hold values from -0.25 to 0.25
- norm1_gain: float32 [512], replicated, may hold values from 0.1 to 1.9
- norm1_bias: float32 [512], replicated, may hold values from -3 to 3
- ffn_in: float32 [512, 2048], P(None, 'head'), may hold values from -0.25 to 0.25
- ffn_out: float32 [2048, 512], P('head'), may hold values from -0.1875 to 0.1875
- norm2_gain: float32 [512], replicated, may hold values from 0.1 to 1.9
- norm2_bias: float32 [512], replicated, may hold values from -3 to 3
Outputs:
- final: float32 [512, 1024], P('head', 'var')
Inputs may be any that keep to these rules, and one draw needn't show every extreme that they name: `emb_weight`: every entry lies within 12 / sqrt(8192) in magnitude, and some entry reaches that bound.
All inputs are finite; a program needn't handle non-finite values.
Results may differ from a plain program's by a relative error of at most 0.0003.
Values sent between devices are 32-bit elements; how exact they have to be, the bound alone decides.
No kernel may reach another device: no remote copies, remote signals or barrier semaphores. Data moves between devices by JAX's collectives and lax.ppermute only.
A program may use at most 64 MiB of HBM per device.

v0:
```python
import math
import jax
import jax.numpy as jnp
from jax import lax
from jax.sharding import PartitionSpec as P

DH = 64
HIGH = lax.Precision.HIGHEST


def product(first_op, second_op):
    return jnp.dot(first_op, second_op, precision=HIGH, preferred_element_type=jnp.float32)


def project_cols(weight, stream):
    return lax.dot_general(
        weight, stream, (((0,), (1,)), ((), ())), precision=HIGH, preferred_element_type=jnp.float32
    )


def layer_norm(stream, scale_gain, shift_bias):
    centre = jnp.mean(stream, axis=-1, keepdims=True)
    spread = stream - centre
    variance = jnp.mean(spread * spread, axis=-1, keepdims=True)
    return spread * lax.rsqrt(variance + 1e-05) * scale_gain + shift_bias


def fold_keys(state, pieces, queries, local_heads):
    key_piece, value_piece = pieces
    piece_len = key_piece.shape[1]
    block_count = max(1, piece_len // 1024)
    while piece_len % block_count:
        block_count += 1
    block_len = piece_len // block_count
    score_scale = 1.0 / math.sqrt(DH)

    def advance(block_num, carry):
        run_max, run_sum, run_acc = carry
        key_block = lax.dynamic_slice_in_dim(
            key_piece, block_num * block_len, block_len, 1
        ).reshape(local_heads, DH, block_len)
        value_block = lax.dynamic_slice_in_dim(
            value_piece, block_num * block_len, block_len, 1
        ).reshape(local_heads, DH, block_len)
        scores = (
            jnp.einsum(
                "hdk,hdq->hkq",
                key_block,
                queries,
                precision=HIGH,
                preferred_element_type=jnp.float32,
            )
            * score_scale
        )
        new_max = jnp.maximum(run_max, jnp.max(scores, axis=1))
        weights = jnp.exp(scores - new_max[:, None, :])
        rescale = jnp.exp(run_max - new_max)
        new_sum = run_sum * rescale + jnp.sum(weights, axis=1)
        new_acc = run_acc * rescale[:, None, :] + jnp.einsum(
            "hdk,hkq->hdq", value_block, weights, precision=HIGH, preferred_element_type=jnp.float32
        )
        return (new_max, new_sum, new_acc)

    return lax.fori_loop(0, block_count, advance, state)


def on_device(
    series,
    emb_weight,
    emb_bias,
    q_weight,
    k_weight,
    v_weight,
    out_weight,
    norm1_gain,
    norm1_bias,
    ffn_in,
    ffn_out,
    norm2_gain,
    norm2_bias,
):
    head_count = lax.axis_size("head")
    head_pos = lax.axis_index("head")
    model_width = emb_bias.shape[0]
    col_count = model_width // head_count
    col_start = head_pos * col_count
    partial_emb = product(series, emb_weight)
    embedded = lax.psum(partial_emb, "head") + emb_bias
    query_count = embedded.shape[0]
    local_heads = q_weight.shape[1] // DH
    queries = project_cols(q_weight, embedded).reshape(local_heads, DH, query_count)
    key_t = project_cols(k_weight, embedded)
    value_t = project_cols(v_weight, embedded)
    start_state = (
        jnp.full((local_heads, query_count), -1e30, jnp.float32),
        jnp.zeros((local_heads, query_count), jnp.float32),
        jnp.zeros((local_heads, DH, query_count), jnp.float32),
    )
    state = fold_keys(
        start_state,
        (
            lax.all_gather(key_t, "var", axis=1, tiled=True),
            lax.all_gather(value_t, "var", axis=1, tiled=True),
        ),
        queries,
        local_heads,
    )
    run_max, run_sum, run_acc = state
    mixed_t = (run_acc / run_sum[:, None, :]).reshape(local_heads * DH, query_count)
    partial_out = lax.dot_general(
        mixed_t,
        out_weight,
        (((0,), (0,)), ((), ())),
        precision=HIGH,
        preferred_element_type=jnp.float32,
    )
    attention = lax.psum(partial_out, "head")
    normed = layer_norm(embedded + attention, norm1_gain, norm1_bias)
    hidden = jax.nn.gelu(product(normed, ffn_in), approximate=False)
    ffn_t = lax.psum_scatter(
        lax.dot_general(
            ffn_out,
            hidden,
            (((0,), (1,)), ((), ())),
            precision=HIGH,
            preferred_element_type=jnp.float32,
        ),
        "head",
        scatter_dimension=0,
        tiled=True,
    )
    resid_t = lax.dynamic_slice_in_dim(normed, col_start, col_count, 1).T + ffn_t
    col_sums = lax.psum((jnp.sum(resid_t, axis=0), jnp.sum(resid_t * resid_t, axis=0)), "head")
    centre = col_sums[0] / model_width
    variance = col_sums[1] / model_width - centre * centre
    gain_part = lax.dynamic_slice_in_dim(norm2_gain, col_start, col_count)
    bias_part = lax.dynamic_slice_in_dim(norm2_bias, col_start, col_count)
    return (resid_t - centre[None, :]) * lax.rsqrt(variance[None, :] + 1e-05) * gain_part[
        :, None
    ] + bias_part[:, None]


def solution(mesh):
    return jax.shard_map(
        on_device,
        mesh=mesh,
        in_specs=(
            P("var", "head"),
            P("head", None),
            P(),
            P(None, "head"),
            P(None, "head"),
            P(None, "head"),
            P("head", None),
            P(),
            P(),
            P(None, "head"),
            P("head", None),
            P(),
            P(),
        ),
        out_specs=P("head", "var"),
        check_vma=False,
    )
```

profile of v0, /device:TPU:0, one launch (start us, length us, event | category | flops | bytes accessed | tf_op | source)
XLA Modules:
  0.0 158.4 jit_solution(4958936107451321450)
XLA Ops:
  6.5 0.0 copy-start
  6.5 0.0 copy-start.5
  6.5 0.0 copy-start.2
  6.5 0.0 copy-start.3
  6.5 0.0 all-reduce.4.cloned.1.call-start
  6.6 1.2 copy-done
  7.8 5.3 %fusion.132 = f32[128,512]{1,0:T(8,128)} fusion(f32[128,2048]{1,0:T(8,128)S(1)} %copy-done, f32[2048,512]{1,0:T(8,128)} %param.14), kind=kOutput, calls=%fused_computation.155 | convolution fusion | flops 1610612736 | bytes 5505024 | tf_op jit(solution)/shard_map/dot_general | solution.py:12
  13.1 0.0 copy-start.4
  13.1 0.0 all-reduce.4.cloned.1.call-update
  13.1 0.0 all-reduce.6.cloned.1.call-start
  13.2 38.4 %all-reduce.4.cloned.1.call-done = f32[128,512]{1,0:T(8,128)} async-done(((f32[128,512]{1,0:T(8,128)}), f32[128,512]{1,0:T(8,128)}) %all-reduce.4.cloned.1.call-update) | async-done | bytes 262160 | tf_op jit(solution)/shard_map/psum | solution.py:88
  51.6 0.0 copy-done.5
  51.6 0.0 copy-done.2
  51.6 0.0 copy-start.1
  51.6 1.4 convolution_bitcast_fusion.2
  53.0 9.8 %all_gather.6 = f32[128,1024]{0,1:T(8,128)S(1)} all-gather(f32[128,128]{0,1:T(8,128)S(1)} %convolution_bitcast_fusion.2), channel_id=1, replica_groups=mesh['var'=8,'head'=4] {'var'}, dimensions={1}, use_global_device_ids=true | all-gather | bytes 589824 | tf_op jit(solution)/shard_map/all_gather | solution.py:102
  62.8 0.2 copy.17
  63.0 0.0 copy-done.3
  63.1 1.5 fusion.62
  64.6 0.0 copy-start.6
  64.6 0.0 copy-start.7
  64.6 1.8 %fusion.131 = (f32[2,128]{1,0:T(2,128)S(1)}, f32[2,1024,128]{2,1,0:T(8,128)S(1)}) fusion(f32[2,64,1024]{2,1,0:T(8,128)S(1)} %bitcast.29, f32[2,64,128]{2,1,0:T(8,128)S(1)} %bitcast.31), kind=kOutput, calls=%fused_computation.154 | convolution fusion | flops 201850624 | bytes 1639424 | tf_op jit(solution)/shard_map/while/body/eval_jaxpr/hdk,hdq->hkq/dot_general | solution.py:46
  66.5 0.2 fusion.1
  66.6 0.0 copy-done.4
  66.6 0.0 copy-done.1
  66.6 0.4 convolution_bitcast_fusion.1
  67.0 9.8 %all_gather.7 = f32[128,1024]{0,1:T(8,128)S(1)} all-gather(f32[128,128]{0,1:T(8,128)S(1)} %convolution_bitcast_fusion.1), channel_id=1, replica_groups=mesh['var'=8,'head'=4] {'var'}, dimensions={1}, use_global_device_ids=true | all-gather | bytes 589824 | tf_op jit(solution)/shard_map/all_gather | solution.py:103
  76.9 0.2 copy.18
  77.1 0.9 fusion
  77.9 2.1 %fusion.133 = f32[128,512]{1,0:T(8,128)} fusion(f32[128,128]{1,0:T(8,128)S(1)} %bitcast.30, f32[128,512]{1,0:T(8,128)} %param.19), kind=kOutput, calls=%fused_computation.156 | convolution fusion | flops 100663296 | bytes 589824 | tf_op jit(solution)/shard_map/dot_general | solution.py:110
  80.0 0.0 all-reduce.6.cloned.1.call-update
  80.0 0.0 reduce-scatter.2.cloned.1.call-start
  80.1 34.6 %all-reduce.6.cloned.1.call-done = f32[128,512]{1,0:T(8,128)} async-done(((f32[128,512]{1,0:T(8,128)}), f32[128,512]{1,0:T(8,128)}) %all-reduce.6.cloned.1.call-update) | async-done | bytes 262160 | tf_op jit(solution)/shard_map/psum | solution.py:117
  114.7 1.1 fusion.130
  115.8 0.2 multiply_reduce_fusion
  116.0 0.0 copy-done.6
  116.0 0.0 copy-done.7
  116.0 0.1 multiply_add_fusion
  116.1 1.9 %fusion.134 = f32[128,512]{1,0:T(8,128)S(1)} fusion(f32[128,512]{1,0:T(8,128)S(1)} %multiply_add_fusion, f32[512,512]{1,0:T(8,128)} %param.22), kind=kOutput, calls=%fused_computation.157 | convolution fusion | flops 402653184 | bytes 1572864 | tf_op jit(solution)/shard_map/dot_general | solution.py:12
  118.1 3.2 %convolution_bitcast_fusion = f32[512,128]{0,1:T(8,128)} fusion(f32[512,512]{1,0:T(8,128)} %param.23, f32[128,512]{1,0:T(8,128)S(1)} %fusion.134), kind=kOutput, calls=%fused_computation.1 | convolution fusion | flops 406847488 | bytes 1572864 | tf_op jit(solution)/shard_map/dot_general | solution.py:121
  121.3 0.0 reduce-scatter.2.cloned.1.call-update
  121.3 0.8 dynamic_slice.14
  122.1 0.8 dynamic_slice.15
  122.8 18.5 %reduce-scatter.2.cloned.1.call-done = f32[128,128]{0,1:T(8,128)} async-done(((f32[512,128]{0,1:T(8,128)}), f32[128,128]{0,1:T(8,128)}) %reduce-scatter.2.cloned.1.call-update) | async-done | bytes 65552 | tf_op jit(solution)/shard_map/reduce_scatter | solution.py:120
  141.3 1.0 fusion.129
  142.3 8.8 %all-reduce = (f32[128]{0:T(128)S(1)}, f32[128]{0:T(128)S(1)}) all-reduce(f32[128]{0:T(128)S(1)} %get-tuple-element.20, f32[128]{0:T(128)S(1)} %get-tuple-element.19), channel_id=1, replica_groups=mesh['var'=8,'head'=4] {'head'}, use_global_device_ids=true, to_apply=%region_10.0 | all-reduce | flops 256 | bytes 2048 | tf_op jit(solution)/shard_map/psum | solution.py:133
  151.1 0.1 multiply_add_fusion.1
  151.2 0.7 copy.19
  (5 shorter events, 0.0 us)
Async XLA Ops:
  6.5 1.2 copy-start
  6.5 45.1 %copy-start.5 = (f32[512]{0:T(512)S(1)}, f32[512]{0:T(512)}, u32[]{:S(2)}) copy-start(f32[512]{0:T(512)} %param.15) | copy-start | bytes 6148
  6.5 45.1 %copy-start.2 = (f32[512,128]{1,0:T(8,128)S(1)}, f32[512,128]{1,0:T(8,128)}, u32[]{:S(2)}) copy-start(f32[512,128]{1,0:T(8,128)} %param.17) | copy-start | bytes 786436
  6.5 56.5 %copy-start.3 = (f32[512,128]{1,0:T(8,128)S(1)}, f32[512,128]{1,0:T(8,128)}, u32[]{:S(2)}) copy-start(f32[512,128]{1,0:T(8,128)} %param.16) | copy-start | bytes 786436
  6.5 45.1 %all-reduce.4.cloned.1.call-start = ((), (), s32[]{:S(2)}) async-start(), calls=%async_computation.1 | async-start | bytes 524288 | tf_op jit(solution)/shard_map/psum | solution.py:88
  13.1 53.5 %copy-start.4 = (f32[512,128]{1,0:T(8,128)S(1)}, f32[512,128]{1,0:T(8,128)}, u32[]{:S(2)}) copy-start(f32[512,128]{1,0:T(8,128)} %param.18) | copy-start | bytes 786436
  13.1 101.6 %all-reduce.6.cloned.1.call-start = ((), (), s32[]{:S(2)}) async-start(), calls=%async_computation.2 | async-start | bytes 524288 | tf_op jit(solution)/shard_map/psum | solution.py:117
  51.6 15.0 %copy-start.1 = (f32[128,512]{1,0:T(8,128)S(1)}, f32[128,512]{1,0:T(8,128)}, u32[]{:S(2)}) copy-start(f32[128,512]{1,0:T(8,128)} %all-reduce.4.cloned.1.call-done) | copy-start | bytes 786436
  64.6 51.4 %copy-start.6 = (f32[512]{0:T(512)S(1)}, f32[512]{0:T(512)}, u32[]{:S(2)}) copy-start(f32[512]{0:T(512)} %param.21) | copy-start | bytes 6148
  64.6 51.4 %copy-start.7 = (f32[512]{0:T(512)S(1)}, f32[512]{0:T(512)}, u32[]{:S(2)}) copy-start(f32[512]{0:T(512)} %param.20) | copy-start | bytes 6148
  80.0 61.3 %reduce-scatter.2.cloned.1.call-start = ((), (), s32[]{:S(2)}) async-start(), calls=%async_computation.3 | async-start | bytes 327680 | tf_op jit(solution)/shard_map/reduce_scatter | solution.py:120
Sparse Core Ops, SparseCore 0:
  13.2 38.3 all-reduce.3
  80.1 34.5 all-reduce.5
  121.4 19.8 reduce-scatter.1
where the time goes:
time: 159 us; the launch traced here: 158 us
  waiting for transfers between devices  91.6 us (58%)
  blocking collectives  28.4 us (18%)
  matrix products  18.6 us (12%)
  between operations  13.3 us (8%)
  local copies, waits for them, and re-layouts  3.84 us (2%)
  other arithmetic  2.62 us (2%)
    psum x1, waiting for transfers between devices, on_device(): embedded = lax.psum(partial_emb, 'head') + emb_bias  38.4 us
    psum x1, waiting for transfers between devices, on_device(): attention = lax.psum(partial_out, 'head')  34.6 us
    reduce_scatter x1, waiting for transfers between devices, on_device(): lax.psum_scatter(lax.dot_general(ffn_out, hidden, (((0,), (1,)), ((), ())...  18.5 us
    all_gather x1, blocking collectives, on_device(): lax.all_gather(key_t, 'var', axis=1, tiled=True)  9.81 us
    all_gather x1, blocking collectives, on_device(): lax.all_gather(value_t, 'var', axis=1, tiled=True)  9.81 us
    psum x1, blocking collectives, on_device(): lax.psum((jnp.sum(resid_t, axis=0), jnp.sum(resid_t * resid_t, axis=0)),...  8.75 us
    dot_general x2, matrix products, product(): jnp.dot(first_op, second_op, precision=HIGH, preferred_element_type=jnp.f...  7.26 us
    dot_general x3, matrix products, project_cols(): lax.dot_general(weight, stream, (((0,), (1,)), ((), ())), precision=HIGH,...  3.35 us
  transfers between devices with their start and end apart: 3, of which 3 were waited for; matrix products, arithmetic and copies ran while one was open for 1% of the time, Pallas kernels for 0%

commit v1 on v0

--- a/solution.py
+++ b/solution.py
@@ -1,3 +1,4 @@
+import functools
 import math
 import jax
 import jax.numpy as jnp
@@ -6,6 +7,28 @@
 
 DH = 64
 HIGH = lax.Precision.HIGHEST
+
+
+def watch_ends_up(work_x, mesh_dim):
+    t_next, finding, known = (lax.axis_size(mesh_dim), lax.axis_index(mesh_dim), work_x.shape[1])
+    newest, extra = (work_x, 1)
+    while extra < t_next:
+        newest = jnp.concatenate(
+            [
+                newest,
+                lax.ppermute(
+                    newest,
+                    axis_name=mesh_dim,
+                    perm=[(pp, (pp - extra) % t_next) for pp in range(t_next)],
+                ),
+            ],
+            axis=1,
+        )
+        extra = 2 * extra
+    return jnp.roll(newest, finding * known, axis=1)
+
+
+step_on_levels_all_on_mesh = functools.partial(watch_ends_up, mesh_dim="var")
 
 
 def product(first_op, second_op):
@@ -98,10 +121,7 @@
     )
     state = fold_keys(
         start_state,
-        (
-            lax.all_gather(key_t, "var", axis=1, tiled=True),
-            lax.all_gather(value_t, "var", axis=1, tiled=True),
-        ),
+        (step_on_levels_all_on_mesh(key_t), lax.all_gather(value_t, "var", axis=1, tiled=True)),
         queries,
         local_heads,
     )

time: 159 us -> 164 us (1.031)
  blocking collectives: 28.4 us -> 22.2 us
  local copies, waits for them, and re-layouts: 3.84 us -> 9.56 us
  starting transfers between devices: 0.12 us -> 3.81 us
  waiting for transfers between devices: 91.6 us -> 94.3 us
    all_gather x1 -> x0, blocking collectives: 9.81 us -> none  [on_device(): lax.all_gather(key_t, 'var', axis=1, tiled=True)]
    unnamed x16 -> x26, local copies, waits for them, and re-layouts: 1.21 us -> 5.1 us
    ppermute x0 -> x3, starting transfers between devices: none -> 3.69 us  [watch_ends_up(): lax.ppermute(newest, axis_name=mesh_dim, perm=[(pp, (pp - extra) % t_next...]
    all_gather x1, blocking collectives: 9.81 us -> 13.4 us  [on_device(): lax.all_gather(value_t, 'var', axis=1, tiled=True)]
    ppermute x0 -> x3, waiting for transfers between devices: none -> 2.63 us  [watch_ends_up(): lax.ppermute(newest, axis_name=mesh_dim, perm=[(pp, (pp - extra) % t_next...]
  transfers between devices with their start and end apart: 3 -> 6, of which waited for: 3 -> 5; matrix products, arithmetic and copies ran while one was open for 1% -> 4% of each run, Pallas kernels for 0% -> 0%
where the time goes in v1:
time: 164 us
  waiting for transfers between devices  94.3 us (58%)
  blocking collectives  22.2 us (14%)
  matrix products  17.9 us (11%)
  between operations  13.3 us (8%)
  local copies, waits for them, and re-layouts  9.56 us (6%)
  starting transfers between devices  3.81 us (2%)
  other arithmetic  2.64 us (2%)
    psum x1, waiting for transfers between devices, on_device(): embedded = lax.psum(partial_emb, 'head') + emb_bias  38.4 us
    psum x1, waiting for transfers between devices, on_device(): attention = lax.psum(partial_out, 'head')  34.7 us
    reduce_scatter x1, waiting for transfers between devices, on_device(): lax.psum_scatter(lax.dot_general(ffn_out, hidden, (((0,), (1,)), ((), ())...  18.5 us
    all_gather x1, blocking collectives, on_device(): lax.all_gather(value_t, 'var', axis=1, tiled=True)  13.4 us
    psum x1, blocking collectives, on_device(): lax.psum((jnp.sum(resid_t, axis=0), jnp.sum(resid_t * resid_t, axis=0)),...  8.84 us
    dot_general x2, matrix products, product(): jnp.dot(first_op, second_op, precision=HIGH, preferred_element_type=jnp.f...  6.03 us
    unnamed x26, local copies, waits for them, and re-layouts  5.1 us
    dot_general x3, matrix products, project_cols(): lax.dot_general(weight, stream, (((0,), (1,)), ((), ())), precision=HIGH,...  4.85 us
  transfers between devices with their start and end apart: 6, of which 5 were waited for; matrix products, arithmetic and copies ran while one was open for 4% of the time, Pallas kernels for 0%

profile of v1, /device:TPU:0, one launch (start us, length us, event | category | flops | bytes accessed | tf_op | source)
XLA Modules:
  0.0 163.7 jit_solution(964568007458419702)
XLA Ops:
  6.5 0.0 all-reduce.4.cloned.1.call-start
  6.6 1.2 copy-done
  7.8 5.3 %fusion.132 = f32[128,512]{1,0:T(8,128)} fusion(f32[128,2048]{1,0:T(8,128)S(1)} %copy-done, f32[2048,512]{1,0:T(8,128)} %param.14), kind=kOutput, calls=%fused_computation.166 | convolution fusion | flops 1610612736 | bytes 5505024 | tf_op jit(solution)/shard_map/dot_general | solution.py:35
  13.1 0.0 all-reduce.4.cloned.1.call-update
  13.1 0.0 all-reduce.6.cloned.1.call-start
  13.2 38.4 %all-reduce.4.cloned.1.call-done = f32[128,512]{1,0:T(8,128)} async-done(((f32[128,512]{1,0:T(8,128)}), f32[128,512]{1,0:T(8,128)}) %all-reduce.4.cloned.1.call-update) | async-done | bytes 262160 | tf_op jit(solution)/shard_map/psum | solution.py:111
  51.6 2.0 %constant_dynamic-update-slice_fusion.7 = (f32[128,2048]{0,1:T(8,128)}, f32[128,128]{0,1:T(8,128)S(1)}) fusion(f32[512,128]{1,0:T(8,128)S(1)} %copy-done.3, f32[128,512]{1,0:T(8,128)} %all-reduce.4.cloned.1.call-done, f32[512]{0:T(512)S(1)} %copy-done.7), kind=kOutput, calls=%fused_computation.124 | convolution fusion | flops 100728832 | bytes 657408 | tf_op jit(solution)/shard_map/dot_general | solution.py:39
  53.6 0.0 collective-permute-start
  53.6 1.5 fusion.62
  55.1 0.4 collective-permute-done
  55.5 2.4 %collective-permute-start.1 = (f32[128,256]{0,1:T(8,128)S(1)}, f32[128,256]{0,1:T(8,128)S(1)}, u32[]{:S(2)}, u32[]{:S(2)}) collective-permute-start(f32[128,256]{0,1:T(8,128)S(1)} %pad_maximum_fusion.1), channel_id=1, source_target_pairs={{0,24},{4,28},{8,0},{12,4},{16,8},{20,12},{24,16},{28,20},{1,25},{... | collective-permute-start | bytes 393224 | tf_op jit(solution)/shard_map/ppermute | solution.py:19
  57.9 0.0 copy-done.5
  57.9 1.3 convolution_bitcast_fusion.1
  59.3 2.3 %collective-permute-done.1 = f32[128,256]{0,1:T(8,128)S(1)} collective-permute-done((f32[128,256]{0,1:T(8,128)S(1)}, f32[128,256]{0,1:T(8,128)S(1)}, u32[]{:S(2)}, u32[]{:S(2)}) %collective-permute-start.1) | collective-permute-done | bytes 131104 | tf_op jit(solution)/shard_map/ppermute | solution.py:19
  61.6 1.3 collective-permute-start.2
  62.8 13.4 %all_gather.3 = f32[128,1024]{0,1:T(8,128)S(1)} all-gather(f32[128,128]{0,1:T(8,128)S(1)} %convolution_bitcast_fusion.1), channel_id=1, replica_groups=mesh['var'=8,'head'=4] {'var'}, dimensions={1}, use_global_device_ids=true | all-gather | bytes 589824 | tf_op jit(solution)/shard_map/all_gather | solution.py:124
  76.2 0.2 copy.17
  76.4 0.0 copy-start.6
  76.4 0.6 constant_dynamic-update-slice_fusion.6
  77.0 0.7 constant_dynamic-update-slice_fusion.5
  77.7 0.0 collective-permute-done.2
  77.7 0.7 constant_dynamic-update-slice_fusion.4
  78.4 0.6 constant_dynamic-update-slice_fusion.3
  79.0 0.6 constant_dynamic-update-slice_fusion.2
  79.7 0.6 constant_dynamic-update-slice_fusion.1
  80.3 0.7 constant_dynamic-update-slice_fusion
  81.0 1.1 constant_dynamic-slice_fusion
  82.2 0.2 copy.16
  82.4 1.8 %fusion.131 = (f32[2,128]{1,0:T(2,128)S(1)}, f32[2,1024,128]{2,1,0:T(8,128)S(1)}) fusion(f32[2,64,1024]{2,1,0:T(8,128)S(1)} %bitcast.29, f32[2,64,128]{2,1,0:T(8,128)S(1)} %bitcast.30), kind=kOutput, calls=%fused_computation.165 | convolution fusion | flops 201850624 | bytes 1639424 | tf_op jit(solution)/shard_map/while/body/eval_jaxpr/hdk,hdq->hkq/dot_general | solution.py:69
  84.2 0.2 fusion.1
  84.4 0.9 fusion
  85.2 1.1 fusion.133
  86.4 0.0 all-reduce.6.cloned.1.call-update
  86.4 0.0 reduce-scatter.2.cloned.1.call-start
  86.4 34.7 %all-reduce.6.cloned.1.call-done = f32[128,512]{1,0:T(8,128)} async-done(((f32[128,512]{1,0:T(8,128)}), f32[128,512]{1,0:T(8,128)}) %all-reduce.6.cloned.1.call-update) | async-done | bytes 262160 | tf_op jit(solution)/shard_map/psum | solution.py:137
  121.1 1.1 fusion.130
  122.2 0.2 multiply_reduce_fusion
  122.4 0.1 multiply_add_fusion
  122.5 0.7 fusion.134
  123.3 3.2 %convolution_bitcast_fusion = f32[512,128]{0,1:T(8,128)} fusion(f32[512,512]{1,0:T(8,128)} %param.23, f32[128,512]{1,0:T(8,128)S(1)} %fusion.134), kind=kOutput, calls=%fused_computation.1 | convolution fusion | flops 406847488 | bytes 1572864 | tf_op jit(solution)/shard_map/dot_general | solution.py:141
  126.5 0.0 reduce-scatter.2.cloned.1.call-update
  126.5 0.8 dynamic_slice.19
  127.3 0.8 dynamic_slice.20
  128.0 18.5 %reduce-scatter.2.cloned.1.call-done = f32[128,128]{0,1:T(8,128)} async-done(((f32[512,128]{0,1:T(8,128)}), f32[128,128]{0,1:T(8,128)}) %reduce-scatter.2.cloned.1.call-update) | async-done | bytes 65552 | tf_op jit(solution)/shard_map/reduce_scatter | solution.py:140
  146.5 1.0 fusion.129
  147.5 8.8 %all-reduce = (f32[128]{0:T(128)S(1)}, f32[128]{0:T(128)S(1)}) all-reduce(f32[128]{0:T(128)S(1)} %get-tuple-element.20, f32[128]{0:T(128)S(1)} %get-tuple-element.19), channel_id=1, replica_groups=mesh['var'=8,'head'=4] {'head'}, use_global_device_ids=true, to_apply=%region_10.11 | all-reduce | flops 256 | bytes 2048 | tf_op jit(solution)/shard_map/psum | solution.py:153
  156.3 0.1 multiply_add_fusion.1
  156.4 0.7 copy.18
  (24 shorter events, 0.1 us)
Async XLA Ops:
  6.5 1.2 copy-start
  6.5 45.1 %copy-start.7 = (f32[512]{0:T(512)S(1)}, f32[512]{0:T(512)}, u32[]{:S(2)}) copy-start(f32[512]{0:T(512)} %param.15) | copy-start | bytes 6148
  6.5 45.1 %copy-start.3 = (f32[512,128]{1,0:T(8,128)S(1)}, f32[512,128]{1,0:T(8,128)}, u32[]{:S(2)}) copy-start(f32[512,128]{1,0:T(8,128)} %param.17) | copy-start | bytes 786436
  6.5 47.0 %copy-start.4 = (f32[512,128]{1,0:T(8,128)S(1)}, f32[512,128]{1,0:T(8,128)}, u32[]{:S(2)}) copy-start(f32[512,128]{1,0:T(8,128)} %param.16) | copy-start | bytes 786436
  6.5 51.4 %copy-start.5 = (f32[512,128]{1,0:T(8,128)S(1)}, f32[512,128]{1,0:T(8,128)}, u32[]{:S(2)}) copy-start(f32[512,128]{1,0:T(8,128)} %param.18) | copy-start | bytes 786436
  6.5 45.0 %all-reduce.4.cloned.1.call-start = ((), (), s32[]{:S(2)}) async-start(), calls=%async_computation.1 | async-start | bytes 524288 | tf_op jit(solution)/shard_map/psum | solution.py:111
  13.1 108.0 %all-reduce.6.cloned.1.call-start = ((), (), s32[]{:S(2)}) async-start(), calls=%async_computation.2 | async-start | bytes 524288 | tf_op jit(solution)/shard_map/psum | solution.py:137
  53.6 1.9 %collective-permute-start = (f32[128,128]{0,1:T(8,128)S(1)}, f32[128,128]{0,1:T(8,128)S(1)}, u32[]{:S(2)}, u32[]{:S(2)}) collective-permute-start(f32[128,128]{0,1:T(8,128)S(1)} %get-tuple-element.41), channel_id=1, source_target_pairs={{0,28},{4,0},{8,4},{12,8},{16,12},{20,16},{24,20},{28,24},{1,29},{... | collective-permute-start | bytes 196616 | tf_op jit(solution)/shard_map/ppermute | solution.py:19
  55.5 6.1 %collective-permute-start.1 = (f32[128,256]{0,1:T(8,128)S(1)}, f32[128,256]{0,1:T(8,128)S(1)}, u32[]{:S(2)}, u32[]{:S(2)}) collective-permute-start(f32[128,256]{0,1:T(8,128)S(1)} %pad_maximum_fusion.1), channel_id=1, source_target_pairs={{0,24},{4,28},{8,0},{12,4},{16,8},{20,12},{24,16},{28,20},{1,25},{... | collective-permute-start | bytes 393224 | tf_op jit(solution)/shard_map/ppermute | solution.py:19
  61.6 16.1 %collective-permute-start.2 = (f32[128,512]{0,1:T(8,128)S(1)}, f32[128,512]{0,1:T(8,128)S(1)}, u32[]{:S(2)}, u32[]{:S(2)}) collective-permute-start(f32[128,512]{0,1:T(8,128)S(1)} %pad_maximum_fusion), channel_id=1, source_target_pairs={{0,16},{4,20},{8,24},{12,28},{16,0},{20,4},{24,8},{28,12},{1,17},{... | collective-permute-start | bytes 786440 | tf_op jit(solution)/shard_map/ppermute | solution.py:19
  76.4 8.8 %copy-start.6 = (f32[128,512]{1,0:T(8,128)S(1)}, f32[128,512]{1,0:T(8,128)}, u32[]{:S(2)}) copy-start(f32[128,512]{1,0:T(8,128)} %param.19) | copy-start | bytes 786436
  78.4 42.7 %copy-start.1 = (f32[128,512]{1,0:T(8,128)S(1)}, f32[128,512]{1,0:T(8,128)}, u32[]{:S(2)}) copy-start(f32[128,512]{1,0:T(8,128)} %all-reduce.4.cloned.1.call-done) | copy-start | bytes 786436
  81.0 41.3 %copy-start.8 = (f32[512]{0:T(512)S(1)}, f32[512]{0:T(512)}, u32[]{:S(2)}) copy-start(f32[512]{0:T(512)} %param.21) | copy-start | bytes 6148
  81.0 41.3 %copy-start.9 = (f32[512]{0:T(512)S(1)}, f32[512]{0:T(512)}, u32[]{:S(2)}) copy-start(f32[512]{0:T(512)} %param.20) | copy-start | bytes 6148
  84.2 38.3 %copy-start.2 = (f32[512,512]{1,0:T(8,128)S(1)}, f32[512,512]{1,0:T(8,128)}, u32[]{:S(2)}) copy-start(f32[512,512]{1,0:T(8,128)} %param.22) | copy-start | bytes 3145732
  86.4 60.1 %reduce-scatter.2.cloned.1.call-start = ((), (), s32[]{:S(2)}) async-start(), calls=%async_computation.3 | async-start | bytes 327680 | tf_op jit(solution)/shard_map/reduce_scatter | solution.py:140
Sparse Core Ops, SparseCore 0:
  13.2 38.3 all-reduce.3
  86.5 34.5 all-reduce.5
  126.6 19.8 reduce-scatter.1
